TPU v7x, 512 devices: a whole 4x8x8 slice. The times are simulated.
512 devices in a mesh: grp: 16 (over z, x_hi), blk: 32 (over x_lo, y, core).
Axes of the slice: x: 4 (x_hi: 2, x_lo: 2; x = x_hi * 2 + x_lo), y: 8, z: 8, core: 2. Of those that a mesh axis runs over, the one named last changes fastest.
Arguments:
- ao_ints: bfloat16 [128, 1504, 1504], P('grp', 'blk'), may hold values from -6 to 6
- v_coeff: bfloat16 [1504, 1344], P(None, 'blk'), may hold values from -0.15625 to 0.15625
- batch_start: int32 [16], replicated, may hold values from 0 to 1496, as said below
- owner_map: int32 [32], replicated, may hold values from 0 to 31, each once
Outputs:
- slab: bfloat16 [128, 1344, 1344], P(None, 'blk', 'grp')
Inputs may be any that keep to these rules, and one draw needn't show every extreme that they name: `batch_start`: distinct multiples of 8; one entry is 0 and one is 1496. `owner_map`: each block number appears once.
All inputs are finite; a program needn't handle non-finite values.
Results may differ from a plain program's by a relative error of at most 0.0049.
Values may be sent and summed in bfloat16 or wider, within the bound.
No kernel may reach another device: no remote copies, remote signals or barrier semaphores. Data moves between devices by JAX's collectives and lax.ppermute only.
A program may use at most 64 MiB of HBM per device.

v0:
```python
import jax
import jax.numpy as jnp
from jax import lax
from jax.sharding import PartitionSpec as P


def in_blocks(x, dim, size):
    before, after = (x.shape[:dim], x.shape[dim + 1 :])
    return jnp.moveaxis(x.reshape(*before, size, -1, *after), dim, 0)


def edges_of(length, count):
    unit = 8 if length >= 8 * count else 1
    return [length // unit * k // count * unit for k in range(1, count)]


def joined_along(pieces, dim):
    pieces = jnp.moveaxis(pieces, 0, dim)
    lengths = pieces.shape
    return pieces.reshape(*lengths[:dim], lengths[dim] * lengths[dim + 1], *lengths[dim + 2 :])


def several_exchanges(x, axis, pieces, split_dim, concat_dim):
    blocks = in_blocks(x, split_dim, lax.axis_size(axis))
    split_at = max(range(1, max(2, blocks.ndim - 1)), key=lambda d: blocks.shape[d])
    gathered = []
    for section in jnp.split(blocks, edges_of(blocks.shape[split_at], pieces), axis=split_at):
        if section.size:
            gathered.append(lax.all_to_all(section, axis, split_axis=0, concat_axis=0, tiled=True))
    return joined_along(jnp.concatenate(gathered, axis=split_at), concat_dim)


def local(ao_ints, v_coeff, batch_start, owner_map):
    sig_rows, lam_rows, ao_count = ao_ints.shape
    ints_flat = ao_ints.reshape(sig_rows * lam_rows, ao_count)
    v_whole = lax.all_gather(v_coeff, "blk", axis=1, tiled=True)
    half_done = jnp.dot(ints_flat, v_whole, preferred_element_type=jnp.float32).astype(jnp.bfloat16)
    half_done = half_done.reshape(sig_rows, lam_rows, -1)
    owned_rows = lax.all_to_all(half_done, "blk", split_axis=2, concat_axis=1, tiled=True)
    third_done = lax.dot_general(
        owned_rows, v_whole, (((1,), (0,)), ((), ())), preferred_element_type=jnp.float32
    ).astype(jnp.bfloat16)
    a_local = third_done.shape[1]
    block_count = owner_map.shape[0]
    block_width = third_done.shape[2] // block_count
    blocked = third_done.reshape(sig_rows, a_local, block_count, block_width)
    ordered = jnp.take(blocked, owner_map, axis=2).reshape(
        sig_rows, a_local, block_count * block_width
    )
    group_count = batch_start.shape[0]
    group_ids = jnp.arange(group_count, dtype=jnp.int32)
    rank = jnp.sum((batch_start[None, :] < batch_start[:, None]).astype(jnp.int32), axis=1)
    source = jnp.sum(
        group_ids[None, :] * (rank[None, :] == group_ids[:, None]).astype(jnp.int32), axis=1
    )
    received = several_exchanges(ordered, "grp", 2, 2, 0)
    item_count = received.shape[1]
    own_width = received.shape[2]
    grouped = received.reshape(group_count, sig_rows, item_count, own_width)
    return jnp.take(grouped, source, axis=0).reshape(group_count * sig_rows, item_count, own_width)


def solution(mesh):
    return jax.shard_map(
        local,
        mesh=mesh,
        in_specs=(P("grp", "blk", None), P(None, "blk"), P(), P()),
        out_specs=P(None, "blk", "grp"),
        check_vma=False,
    )
```

profile of v0, /device:TPU:8, one launch (start us, length us, event | category | flops | bytes accessed | tf_op | source)
XLA Modules:
  0.0 247.0 jit_solution(10376196617440628879)
XLA Ops:
  7.3 1.6 copy.37
  9.4 73.7 %all-gather.3.cloned.1.call-done = bf16[32,42,1504]{2,1,0:T(8,128)(2,1)} async-done(((bf16[1,42,1504]{2,1,0:T(8,128)(2,1)}), bf16[32,42,1504]{2,1,0:T(8,128)(2,1)}) %all-gather.3.cloned.1.call-update) | async-done | bytes 4042768 | tf_op jit(solution)/shard_map/all_gather | solution.py:36
  83.1 7.5 %reshape.64 = bf16[1344,1504]{1,0:T(8,128)(2,1)} reshape(bf16[32,42,1504]{2,1,0:T(8,128)(2,1)} %all-gather.3.cloned.1.call-done) | data formatting | bytes 8085504
  90.6 5.5 %convolution_convert_fusion.1 = bf16[376,1344]{0,1:T(8,128)(2,1)} fusion(bf16[376,1504]{1,0:T(8,128)(2,1)S(1)} %reshape.43, bf16[1344,1504]{1,0:T(8,128)(2,1)} %reshape.64), kind=kOutput, calls=%fused_computation.3 | convolution fusion | flops 1520580096 | bytes 6184448 | tf_op jit(solution)/shard_map/dot_general | solution.py:37
  96.1 3.8 %reshape.66 = bf16[8,47,1344]{1,0,2:T(8,128)(2,1)S(1)} reshape(bf16[376,1344]{0,1:T(8,128)(2,1)} %convolution_convert_fusion.1) | data formatting | bytes 2021376 | tf_op jit(solution)/shard_map/reshape | solution.py:38
  99.9 4.9 %reshape.70 = bf16[32,2,7896]{2,1,0:T(2,128)(2,1)} reshape(bf16[1344,8,47]{2,1,0:T(8,128)(2,1)S(1)} %bitcast.31) | data formatting | bytes 2021376
  104.8 7.7 %all-to-all-start = ((bf16[32,2,7896]{2,1,0:T(2,128)(2,1)}), bf16[32,2,7896]{2,1,0:T(2,128)(2,1)}, u32[]{:S(2)}, u32[]{:S(2)}) async-start(bf16[32,2,7896]{2,1,0:T(2,128)(2,1)} %reshape.70), calls=%async_computation | async-start | bytes 2031616 | tf_op jit(solution)/shard_map/all_to_all | solution.py:39
  112.9 7.5 %reshape.65 = bf16[1344,1504,1]{1,0,2:T(8,128)(2,1)} reshape(bf16[32,42,1504]{2,1,0:T(8,128)(2,1)} %all-gather.3.cloned.1.call-done) | data formatting | bytes 8085504
  120.3 20.5 %all-to-all-done = bf16[32,2,7896]{2,1,0:T(2,128)(2,1)} async-done(((bf16[32,2,7896]{2,1,0:T(2,128)(2,1)}), bf16[32,2,7896]{2,1,0:T(2,128)(2,1)}, u32[]{:S(2)}, u32[]{:S(2)}) %all-to-all-start) | async-done | bytes 1010720 | tf_op jit(solution)/shard_map/all_to_all | solution.py:39
  140.9 5.5 %reshape.71 = bf16[1344,8,47]{2,1,0:T(8,128)(2,1)S(1)} reshape(bf16[32,2,7896]{2,1,0:T(2,128)(2,1)} %all-to-all-done) | data formatting | bytes 2021376
  146.4 2.3 copy.51
  148.7 5.7 %reshape.67 = bf16[8,1504,42]{1,2,0:T(8,128)(2,1)S(1)} reshape(bf16[8,32,47,42]{2,1,3,0:T(8,128)(2,1)} %copy.51) | data formatting | bytes 2021376 | tf_op jit(solution)/shard_map/all_to_all | solution.py:39
  154.3 4.2 %convolution_convert_fusion = bf16[8,42,1344]{2,1,0:T(8,128)(2,1)S(1)} fusion(bf16[8,1504,42]{1,2,0:T(8,128)(2,1)S(1)} %reshape.67, bf16[1344,1504,1]{1,0,2:T(8,128)(2,1)} %reshape.65), kind=kOutput, calls=%fused_computation.2 | convolution fusion | flops 1358816256 | bytes 5956608 | tf_op jit(solution)/shard_map/dot_general | solution.py:40
  158.5 8.9 %reshape.69 = bf16[8,42,32,42]{3,2,1,0:T(8,128)(2,1)} reshape(bf16[8,42,1344]{2,1,0:T(8,128)(2,1)S(1)} %convolution_convert_fusion) | data formatting | bytes 1806336 | tf_op jit(solution)/shard_map/reshape | solution.py:46
  167.5 5.0 %copy.44 = bf16[8,42,32,42]{3,0,2,1:T(8,128)(2,1)S(1)} copy(bf16[8,42,32,42]{3,2,1,0:T(8,128)(2,1)} %reshape.69) | data formatting | bytes 1806336 | tf_op jit(solution)/shard_map/reshape | solution.py:46
  172.4 3.0 %gather_fusion = bf16[32,8,42,42]{3,1,2,0:T(8,128)(2,1)} fusion(bf16[8,42,32,42]{3,0,2,1:T(8,128)(2,1)S(1)} %copy.44, s32[1024]{0:T(1024)S(1)} %pad_clamp_fusion.1), kind=kCustom, calls=%fused_computation | custom fusion | bytes 1806464 | tf_op jit(solution)/shard_map/jit(_take)/gather | solution.py:47
  175.4 2.5 %copy.45 = bf16[8,42,32,42]{3,2,1,0:T(8,128)(2,1)S(1)} copy(bf16[8,42,32,42]{3,0,1,2:T(8,128)(2,1)} %bitcast.30) | data formatting | bytes 1806336 | tf_op jit(solution)/shard_map/jit(_take)/gather | solution.py:47
  177.9 2.4 gather.13
  180.3 1.8 fusion
  182.9 9.5 %all-to-all-start.1 = ((bf16[16,8,16,84]{3,1,2,0:T(8,128)(2,1)}), bf16[16,8,16,84]{3,1,2,0:T(8,128)(2,1)S(1)}, u32[]{:S(2)}, u32[]{:S(2)}) async-start(bf16[16,8,16,84]{3,1,2,0:T(8,128)(2,1)} %split.8), calls=%async_computation.1 | async-start | bytes 1048576 | tf_op jit(solution)/shard_map/all_to_all | solution.py:29
  193.4 16.7 %all-to-all-done.1 = bf16[16,8,16,84]{3,1,2,0:T(8,128)(2,1)S(1)} async-done(((bf16[16,8,16,84]{3,1,2,0:T(8,128)(2,1)}), bf16[16,8,16,84]{3,1,2,0:T(8,128)(2,1)S(1)}, u32[]{:S(2)}, u32[]{:S(2)}) %all-to-all-start.1) | async-done | bytes 344096 | tf_op jit(solution)/shard_map/all_to_all | solution.py:29
  210.1 3.6 %all-to-all-start.2 = ((bf16[16,8,26,84]{3,1,2,0:T(8,128)(2,1)}), bf16[16,8,26,84]{3,1,2,0:T(8,128)(2,1)S(1)}, u32[]{:S(2)}, u32[]{:S(2)}) async-start(bf16[16,8,26,84]{3,1,2,0:T(8,128)(2,1)} %split.9), calls=%async_computation.2 | async-start | bytes 1703936 | tf_op jit(solution)/shard_map/all_to_all | solution.py:29
  214.3 23.0 %all-to-all-done.2 = bf16[16,8,26,84]{3,1,2,0:T(8,128)(2,1)S(1)} async-done(((bf16[16,8,26,84]{3,1,2,0:T(8,128)(2,1)}), bf16[16,8,26,84]{3,1,2,0:T(8,128)(2,1)S(1)}, u32[]{:S(2)}, u32[]{:S(2)}) %all-to-all-start.2) | async-done | bytes 559136 | tf_op jit(solution)/shard_map/all_to_all | solution.py:29
  238.6 1.5 copy.48
  (25 shorter events, 5.2 us)
Async XLA Ops:
  6.5 76.6 %all-gather.3.cloned.1.call-start = ((), (), s32[]{:S(2)}) async-start(), calls=%async_computation.3 | async-start | bytes 4866048 | tf_op jit(solution)/shard_map/all_gather | solution.py:36
  104.8 7.7 %copy-start = (s32[32]{0:T(128)S(1)}, s32[32]{0:T(128)}, u32[]{:S(2)}) copy-start(s32[32]{0:T(128)} %param.7) | copy-start | bytes 388
  104.8 36.0 %all-to-all-start = ((bf16[32,2,7896]{2,1,0:T(2,128)(2,1)}), bf16[32,2,7896]{2,1,0:T(2,128)(2,1)}, u32[]{:S(2)}, u32[]{:S(2)}) async-start(bf16[32,2,7896]{2,1,0:T(2,128)(2,1)} %reshape.70), calls=%async_computation | async-start | bytes 2031616 | tf_op jit(solution)/shard_map/all_to_all | solution.py:39
  182.9 27.2 %all-to-all-start.1 = ((bf16[16,8,16,84]{3,1,2,0:T(8,128)(2,1)}), bf16[16,8,16,84]{3,1,2,0:T(8,128)(2,1)S(1)}, u32[]{:S(2)}, u32[]{:S(2)}) async-start(bf16[16,8,16,84]{3,1,2,0:T(8,128)(2,1)} %split.8), calls=%async_computation.1 | async-start | bytes 1048576 | tf_op jit(solution)/shard_map/all_to_all | solution.py:29
  192.4 21.3 %copy-start.1 = (s32[16]{0:T(128)S(1)}, s32[16]{0:T(128)}, u32[]{:S(2)}) copy-start(s32[16]{0:T(128)} %param.6) | copy-start | bytes 196
  210.1 27.2 %all-to-all-start.2 = ((bf16[16,8,26,84]{3,1,2,0:T(8,128)(2,1)}), bf16[16,8,26,84]{3,1,2,0:T(8,128)(2,1)S(1)}, u32[]{:S(2)}, u32[]{:S(2)}) async-start(bf16[16,8,26,84]{3,1,2,0:T(8,128)(2,1)} %split.9), calls=%async_computation.2 | async-start | bytes 1703936 | tf_op jit(solution)/shard_map/all_to_all | solution.py:29
Sparse Core Ops, SparseCore 0:
  9.5 73.5 all-gather.2
where the time goes:
time: 248 us; the launch traced here: 247 us
  waiting for transfers between devices  135 us (54%)
  local copies, waits for them, and re-layouts  65.6 us (26%)
  starting transfers between devices  20.8 us (8%)
  between operations  13.6 us (5%)
  matrix products  9.71 us (4%)
  other arithmetic  2.65 us (1%)
    all_gather x1, waiting for transfers between devices, local(): v_whole = lax.all_gather(v_coeff, 'blk', axis=1, tiled=True)  73.7 us
    all_to_all x2, waiting for transfers between devices, several_exchanges(): lax.all_to_all(section, axis, split_axis=0, concat_axis=0, tiled=True)  39.7 us
    unnamed x9, local copies, waits for them, and re-layouts  27 us
    all_to_all x1, waiting for transfers between devices, local(): lax.all_to_all(half_done, 'blk', split_axis=2, concat_axis=1, tiled=True)  20.5 us
    reshape x2, local copies, waits for them, and re-layouts, local(): blocked = third_done.reshape(sig_rows, a_local, block_count, block_width)  13.9 us
    all_to_all x2, starting transfers between devices, several_exchanges(): lax.all_to_all(section, axis, split_axis=0, concat_axis=0, tiled=True)  13.1 us
    all_to_all x2, local copies, waits for them, and re-layouts, local(): lax.all_to_all(half_done, 'blk', split_axis=2, concat_axis=1, tiled=True)  7.93 us
    gather x3, local copies, waits for them, and re-layouts, local(): jnp.take(blocked, owner_map, axis=2)  7.84 us
  transfers between devices with their start and end apart: 4, of which 4 were waited for; matrix products, arithmetic and copies ran while one was open for 5% of the time, Pallas kernels for 0%

commit v1 on v0

v1 whole, which is shorter than its diff:
```python
import functools

import jax
import jax.numpy as jnp
from jax import lax
from jax.experimental import pallas as pl
from jax.experimental.pallas import tpu as pltpu
from jax.sharding import PartitionSpec as P


BF = jnp.bfloat16
F32 = jnp.float32
NX, NY, NZ, NC = 2, 8, 8, 2
XN = 4


def blk_of(xl, y, c):
    return (xl * NY + y) * NC + c


def y_groups():
    return [[blk_of(xl, y, c) for y in range(NY)] for xl in range(NX) for c in range(NC)]


def xy_groups():
    return [[blk_of(xl, y, c) for xl in range(NX) for y in range(NY)] for c in range(NC)]


def core_swap():
    return [(i, i ^ 1) for i in range(NX * NY * NC)]


def x_shift(d):
    pairs = []
    for z in range(NZ):
        for x in range(XN):
            to = (x + d) % XN
            for y in range(NY):
                for c in range(NC):
                    src = (z * 2 + x // 2) * 32 + blk_of(x % 2, y, c)
                    dst = (z * 2 + to // 2) * 32 + blk_of(to % 2, y, c)
                    pairs.append((src, dst))
    return pairs


def nn(a, b):
    return lax.dot_general(a, b, (((1,), (0,)), ((), ())), preferred_element_type=F32)


def nt(a, b):
    return lax.dot_general(a, b, (((1,), (1,)), ((), ())), preferred_element_type=F32)


def iota(shape, dim):
    return lax.broadcasted_iota(jnp.int32, shape, dim)


def spread(rows, lam, lam_pad, o_store):
    total = rows.shape[1]
    width_in, width_out = 8 * lam, 8 * lam_pad
    for i in range(total // width_in):
        lo = width_in * i // 128 * 128
        off = width_in * i - lo
        hi = min(lo + (off + width_in + 127) // 128 * 128, total)
        window = rows[:, lo:hi]
        shape = (hi - lo, width_out)
        r, c = iota(shape, 0), iota(shape, 1)
        block = c // lam_pad
        within = c - block * lam_pad
        pick = (within < lam) & (r == off + block * lam + within)
        o_store(i * width_out, nn(window, jnp.where(pick, 1.0, 0.0).astype(BF)).astype(BF))


def pad_v_kernel(lam, lam_pad, v_ref, o_ref):
    def store(at, val):
        o_ref[:, at : at + val.shape[1]] = val

    spread(v_ref[...], lam, lam_pad, store)


def split_kernel(v_ref, lo_ref, hi_ref):
    blocks, width, _ = v_ref.shape
    pad = lo_ref.shape[0] // (blocks // 2)
    for n, ref in enumerate((lo_ref, hi_ref)):
        for i in range(blocks // 2):
            ref[i * pad + width // 16 * 16 : (i + 1) * pad, :] = jnp.zeros((pad - width // 16 * 16, ref.shape[1]), BF)
            ref[i * pad : i * pad + width, :] = v_ref[n * blocks // 2 + i]


def arrange_kernel(lam, lam_pad, core_ref, own_ref, oth_ref, o_ref):
    n_in = own_ref.shape[0]
    n_out = o_ref.shape[1]
    shape = (n_out, n_in)
    r, c = iota(shape, 0), iota(shape, 1)
    s = r // lam_pad
    l = r - s * lam_pad
    perm = jnp.where((l < lam) & (c == l * 8 + s), 1.0, 0.0).astype(BF)
    core = core_ref[0]
    for ref, at in ((own_ref, core), (oth_ref, 1 - core)):
        rows = nn(perm, ref[...]).astype(BF)

        def store(col, val, at=at):
            o_ref[at, :, col : col + val.shape[1]] = val

        spread(rows, lam, lam_pad, store)


def half_kernel(pad, xl_ref, a_ref, v0_ref, v1_ref, v2_ref, v3_ref, o_ref, w_ref, g_ref):
    xl = xl_ref[0]
    half = NY * pad
    for n, ref in enumerate((v0_ref, v1_ref, v2_ref, v3_ref)):
        x = xl if n < 2 else 1 - xl
        at = pl.multiple_of(x * half + n % 2 * (half // 2), half // 2)
        w_ref[pl.ds(at, half // 2), :] = ref[...]
    rows = 16
    shape = (rows, 8 * pad)
    block = iota(shape, 1) // pad
    masks = {b: (block & b) != 0 for b in (4, 2, 1)}
    for x in range(NX):
        w = w_ref[x * half : (x + 1) * half, :]
        for core in range(NC):
            g_ref[...] = nt(a_ref[core], w)
            for l0 in range(0, pad, rows):
                g = [g_ref[s * pad + l0 : s * pad + l0 + rows, :] for s in range(8)]
                for b in (4, 2, 1):
                    new = list(g)
                    for s in range(8):
                        if s & b == 0:
                            lo, hi = g[s], g[s | b]
                            new[s] = jnp.where(masks[b], pltpu.roll(hi, pad * b, 1), lo)
                            new[s | b] = jnp.where(masks[b], hi, pltpu.roll(lo, 8 * pad - pad * b, 1))
                    g = new
                for y in range(NY):
                    o_ref[x * NY + y, core * pad + l0 : core * pad + l0 + rows, :] = g[y].astype(BF)


def third_kernel(pad, where_ref, owner_ref, r_ref, *refs):
    v_refs, o_ref, w_ref, pos_ref = refs[:8], refs[8], refs[9], refs[10]
    blocks = NX * NY * NC
    for p in range(blocks):
        pos_ref[owner_ref[p]] = p
    xl, core = where_ref[0], where_ref[1]
    for n, ref in enumerate(v_refs):
        c = core if n < 4 else 1 - core
        x = xl if n % 4 < 2 else 1 - xl
        for i in range(NY // 2):
            k = (x * NY + n % 2 * (NY // 2) + i) * NC + c
            at = pl.multiple_of(pos_ref[k] * pad, pad)
            w_ref[pl.ds(at, pad), :] = ref[i * pad : (i + 1) * pad, :]
    r = r_ref[...].reshape(r_ref.shape[0] * r_ref.shape[1], r_ref.shape[2])
    per = o_ref.shape[1]
    for m in range(0, o_ref.shape[0], 4):
        out = nn(w_ref[m * per : (m + 4) * per, :], r).astype(BF)
        o_ref[m : m + 4] = out.reshape(4, per, out.shape[1])


def gather_kernel(pad, start_ref, x_ref, o_ref, t_ref):
    groups, rows_in, lanes = x_ref.shape
    n_a, n_b, _ = o_ref.shape
    shape = (n_a * 8, lanes)
    r, c = iota(shape, 0), iota(shape, 1)
    a = r // 8
    pick = jnp.where(c == (r - a * 8) * pad + a, 1.0, 0.0).astype(BF)
    fill = jnp.zeros((128 - rows_in, lanes), BF)
    for g in range(groups):
        rank = jnp.int32(0)
        for h in range(groups):
            rank = rank + (start_ref[h] < start_ref[g]).astype(jnp.int32)
        t_ref[rank] = nt(pick, jnp.concatenate([x_ref[g], fill], axis=0)).astype(BF).astype(F32)
    shape = (n_b, 128)
    r, c = iota(shape, 0), iota(shape, 1)
    half = n_b // 2
    tight = jnp.where(c == jnp.where(r < half, r, r - half + pad), 1.0, 0.0).astype(BF)
    for a in range(n_a):
        tile = t_ref[:, a * 8 : (a + 1) * 8, :].reshape(groups * 8, 128).astype(BF)
        o_ref[a] = nt(tight, tile).astype(BF)


SMEM = pl.BlockSpec(memory_space=pltpu.SMEM)
VMEM = pl.BlockSpec(memory_space=pltpu.VMEM)


def call(kernel, out_shape, n_smem, n_vmem, scratch=(), flops=0, moved=0):
    return pl.pallas_call(
        kernel,
        out_shape=jax.ShapeDtypeStruct(out_shape, BF),
        in_specs=[SMEM] * n_smem + [VMEM] * n_vmem,
        out_specs=VMEM,
        scratch_shapes=list(scratch),
        cost_estimate=pl.CostEstimate(flops=flops, bytes_accessed=moved, transcendentals=0),
    )


def local(ao_ints, v_coeff, batch_start, owner_map):
    sig, lam, nao = ao_ints.shape
    width = v_coeff.shape[1]
    pad = 48
    nblk, ngrp = owner_map.shape[0], batch_start.shape[0]
    kdim = nblk * pad
    me = lax.axis_index("blk").astype(jnp.int32)
    core, xl = me % NC, me // (NY * NC)
    ao_rows = ao_ints.transpose(1, 0, 2).reshape(lam * sig, nao)
    ao_other = lax.ppermute(ao_rows, "blk", core_swap())
    v_pad = call(functools.partial(pad_v_kernel, lam, pad), (width, kdim), 0, 1)(v_coeff.T)
    v_y = lax.all_gather(v_pad, "blk", axis=0, axis_index_groups=y_groups())
    part = jax.ShapeDtypeStruct((NY // 2 * pad, kdim), BF)
    v_y0, v_y1 = pl.pallas_call(
        split_kernel, out_shape=(part, part), in_specs=[VMEM], out_specs=(VMEM, VMEM), name="split"
    )(v_y)
    v_x0 = lax.ppermute(v_y0, ("grp", "blk"), x_shift(1))
    v_x1 = lax.ppermute(v_y1, ("grp", "blk"), x_shift(-1))
    mine = (v_y0, v_y1, v_x0, v_x1)
    ao = call(
        functools.partial(arrange_kernel, lam, pad), (NC, sig * pad, kdim), 1, 2,
        flops=6 * 10**9, moved=5 * 10**6,
    )(core.reshape(1), ao_rows, ao_other)
    halves = call(
        functools.partial(half_kernel, pad), (NX * NY, NC * pad, sig * pad), 1, 5,
        scratch=[pltpu.VMEM((NX * NY * pad, kdim), BF), pltpu.VMEM((sig * pad, NY * pad), F32)],
        flops=2 * 10**9, moved=6 * 10**6,
    )(xl.reshape(1), ao, *mine)
    owned = lax.all_to_all(halves, "blk", split_axis=0, concat_axis=0, tiled=True, axis_index_groups=xy_groups())
    swapped = [lax.ppermute(v, "blk", core_swap()) for v in mine]
    third = call(
        functools.partial(third_kernel, pad), (ngrp, nblk // ngrp * pad, sig * pad), 2, 9,
        scratch=[pltpu.VMEM((kdim, kdim), BF), pltpu.SMEM((nblk,), jnp.int32)],
        flops=2 * 10**9, moved=7 * 10**6,
    )(jnp.stack([xl, core]), owner_map, owned, *mine, *swapped)
    received = lax.all_to_all(third, "grp", split_axis=0, concat_axis=0, tiled=True)
    out = call(
        functools.partial(gather_kernel, pad), (width, nblk // ngrp * width, ngrp * sig), 1, 1,
        scratch=[pltpu.VMEM((ngrp, width * 8, 128), F32)],
        flops=10**9, moved=2 * 10**6,
    )(batch_start, received)
    return out.transpose(2, 0, 1)


def solution(mesh):
    return jax.shard_map(
        local,
        mesh=mesh,
        in_specs=(P("grp", "blk", None), P(None, "blk"), P(), P()),
        out_specs=P(None, "blk", "grp"),
        check_vma=False,
    )
```

time: 248 us -> 146 us (0.59)
  the two profiles are of different devices: /device:TPU:8 before, /device:TPU:24 now
where the time goes in v1:
time: 146 us; the launch traced here: 145 us
  blocking collectives  73 us (50%)
  Pallas kernels  28.3 us (19%)
  starting transfers between devices  25.4 us (17%)
  waiting for transfers between devices  13 us (9%)
  local copies, waits for them, and re-layouts  4.8 us (3%)
    all_to_all x1, blocking collectives, local(): lax.all_to_all(third, 'grp', split_axis=0, concat_axis=0, tiled=True)  43.1 us
    all_gather x1, blocking collectives, local(): v_y = lax.all_gather(v_pad, 'blk', axis=0, axis_index_groups=y_groups())  29.9 us
    all_to_all x1, waiting for transfers between devices, local(): lax.all_to_all(halves, 'blk', split_axis=0, concat_axis=0, tiled=True, ax...  11.5 us
    ppermute x4, starting transfers between devices, local(): swapped = [lax.ppermute(v, 'blk', core_swap()) for v in mine]  8.65 us
    all_to_all x1, starting transfers between devices, local(): lax.all_to_all(halves, 'blk', split_axis=0, concat_axis=0, tiled=True, ax...  7.79 us
    pallas_call x1, Pallas kernels, local(): call(functools.partial(third_kernel, pad), (ngrp, nblk // ngrp * pad, sig...  6.65 us
    pallas_call x1, Pallas kernels, local(): call(functools.partial(half_kernel, pad), (NX * NY, NC * pad, sig * pad),...  6.39 us
    pallas_call x1, Pallas kernels, local(): call(functools.partial(arrange_kernel, lam, pad), (NC, sig * pad, kdim),...  6.06 us
  transfers between devices with their start and end apart: 8, of which 3 were waited for; matrix products, arithmetic and copies ran while one was open for 0% of the time, Pallas kernels for 7%

profile of v1, /device:TPU:24, one launch (start us, length us, event | category | flops | bytes accessed | tf_op | source)
XLA Modules:
  0.0 145.3 jit_solution(13626613664871184402)
XLA Ops:
  0.0 1.9 %collective-permute-start = (bf16[376,1504]{1,0:T(8,128)(2,1)}, bf16[376,1504]{1,0:T(8,128)(2,1)S(1)}, u32[]{:S(2)}, u32[]{:S(2)}) collective-permute-start(bf16[376,1504]{1,0:T(8,128)(2,1)} %bitcast.10), channel_id=1, source_target_pairs={{0,1},{1,0},{2,3},{3,2},{4,5},{5,4},{6,7},{7,6},{8,9},{9,8},{10,11... | collective-permute-start | bytes 3393032 | tf_op jit(solution)/shard_map/ppermute | solution.py:203
  1.9 2.0 %shard_map.47 = bf16[42,1536]{1,0:T(8,128)(2,1)} custom-call(bf16[42,1504]{1,0:T(8,128)(2,1)} %bitcast.9), custom_call_target="tpu_custom_call" | custom-call | tf_op jit(solution)/shard_map/pallas_call | solution.py:204
  3.9 29.9 %all-gather.1.v_ref = bf16[8,42,1536]{2,1,0:T(8,128)(2,1)} all-gather(bf16[1,42,1536]{2,1,0:T(8,128)(2,1)} %bitcast.8), channel_id=2, replica_groups={{0,2,4,6,8,10,12,14},{1,3,5,7,9,11,13,15},{16,18,20,22,24,26,28,30},{17..., dimensions={0}, use_global_device_ids=true | all-gather | bytes 1161216 | tf_op jit(solution)/shard_map/all_gather | solution.py:205
  33.8 2.3 %split.1 = (bf16[192,1536]{1,0:T(8,128)(2,1)}, bf16[192,1536]{1,0:T(8,128)(2,1)}) custom-call(bf16[8,42,1536]{2,1,0:T(8,128)(2,1)} %all-gather.1.v_ref), custom_call_target="tpu_custom_call" | custom-call | tf_op jit(solution)/shard_map/split/pallas_call | solution.py:207
  36.2 3.2 %collective-permute-start.1 = (bf16[192,1536]{1,0:T(8,128)(2,1)}, bf16[192,1536]{1,0:T(8,128)(2,1)S(1)}, u32[]{:S(2)}, u32[]{:S(2)}) collective-permute-start(bf16[192,1536]{1,0:T(8,128)(2,1)} %get-tuple-element.7.v0_ref.refs_0_), channel_id=1, source_target_pairs={{0,16},{1,17},{2,18},{3,19},{4,20},{5,21},{6,22},{7,23},{8,24},{9,... | collective-permute-start | bytes 1769480 | tf_op jit(solution)/shard_map/ppermute | solution.py:210
  39.4 3.8 %collective-permute-start.2 = (bf16[192,1536]{1,0:T(8,128)(2,1)}, bf16[192,1536]{1,0:T(8,128)(2,1)S(1)}, u32[]{:S(2)}, u32[]{:S(2)}) collective-permute-start(bf16[192,1536]{1,0:T(8,128)(2,1)} %get-tuple-element.8.v1_ref.refs_1_), channel_id=1, source_target_pairs={{0,48},{1,49},{2,50},{3,51},{4,52},{5,53},{6,54},{7,55},{8,56},{9,... | collective-permute-start | bytes 1769480 | tf_op jit(solution)/shard_map/ppermute | solution.py:211
  43.3 1.1 copy-done.1
  44.3 6.1 %shard_map.46.a_ref = bf16[2,384,1536]{2,1,0:T(8,128)(2,1)} custom-call(s32[1]{0:T(128)} %bitcast.1.core_ref, bf16[376,1504]{1,0:T(8,128)(2,1)} %bitcast.11, bf16[376,1504]{1,0:T(8,128)(2,1)} %copy-done.1), custom_call_target="tpu_custom_call" | custom-call | flops 6000000000 | bytes 5000000 | tf_op jit(solution)/shard_map/pallas_call | solution.py:213
  50.6 1.3 collective-permute-done.2.v3_ref.refs_3_
  51.9 0.8 copy-done.6
  52.7 6.4 %shard_map.48 = bf16[16,96,384]{2,1,0:T(8,128)(2,1)} custom-call(s32[1]{0:T(128)} %bitcast.xl_ref, bf16[2,384,1536]{2,1,0:T(8,128)(2,1)} %shard_map.46.a_ref, bf16[192,1536]{1,0:T(8,128)(2,1)} %get-tuple-element.7.v0_ref.refs_0_, bf16[192,1536]{1,0:T(8,128)(2,1)} %get-tuple-element.8.v1_ref.refs_1_, bf16[192,1536]{1,0:T(8,128)(2,1)} %copy-done.4, ...), custom_call_target="tpu_custom_call" | custom-call | flops 2000000000 | bytes 6000000 | tf_op jit(solution)/shard_map/pallas_call | solution.py:217
  59.1 7.8 %all-to-all-start = ((bf16[16,96,384]{2,1,0:T(8,128)(2,1)}), bf16[16,96,384]{2,1,0:T(8,128)(2,1)S(1)}, u32[]{:S(2)}, u32[]{:S(2)}) async-start(bf16[16,96,384]{2,1,0:T(8,128)(2,1)} %shard_map.48), calls=%async_computation | async-start | bytes 2359296 | tf_op jit(solution)/shard_map/all_to_all | solution.py:222
  66.9 1.9 %collective-permute-start.3 = (bf16[192,1536]{1,0:T(8,128)(2,1)S(1)}, bf16[192,1536]{1,0:T(8,128)(2,1)S(1)}, u32[]{:S(2)}, u32[]{:S(2)}) collective-permute-start(bf16[192,1536]{1,0:T(8,128)(2,1)S(1)} %copy-done.2), channel_id=1, source_target_pairs={{0,1},{1,0},{2,3},{3,2},{4,5},{5,4},{6,7},{7,6},{8,9},{9,8},{10,11... | collective-permute-start | bytes 1769480 | tf_op jit(solution)/shard_map/ppermute | solution.py:223
  68.8 2.4 %collective-permute-start.4 = (bf16[192,1536]{1,0:T(8,128)(2,1)S(1)}, bf16[192,1536]{1,0:T(8,128)(2,1)S(1)}, u32[]{:S(2)}, u32[]{:S(2)}) collective-permute-start(bf16[192,1536]{1,0:T(8,128)(2,1)S(1)} %copy-done.3), channel_id=1, source_target_pairs={{0,1},{1,0},{2,3},{3,2},{4,5},{5,4},{6,7},{7,6},{8,9},{9,8},{10,11... | collective-permute-start | bytes 1769480 | tf_op jit(solution)/shard_map/ppermute | solution.py:223
  71.3 1.9 %collective-permute-start.5 = (bf16[192,1536]{1,0:T(8,128)(2,1)S(1)}, bf16[192,1536]{1,0:T(8,128)(2,1)S(1)}, u32[]{:S(2)}, u32[]{:S(2)}) collective-permute-start(bf16[192,1536]{1,0:T(8,128)(2,1)S(1)} %copy-done.5), channel_id=1, source_target_pairs={{0,1},{1,0},{2,3},{3,2},{4,5},{5,4},{6,7},{7,6},{8,9},{9,8},{10,11... | collective-permute-start | bytes 1769480 | tf_op jit(solution)/shard_map/ppermute | solution.py:223
  73.2 2.4 %collective-permute-start.6 = (bf16[192,1536]{1,0:T(8,128)(2,1)S(1)}, bf16[192,1536]{1,0:T(8,128)(2,1)}, u32[]{:S(2)}, u32[]{:S(2)}) collective-permute-start(bf16[192,1536]{1,0:T(8,128)(2,1)S(1)} %copy-done.7), channel_id=1, source_target_pairs={{0,1},{1,0},{2,3},{3,2},{4,5},{5,4},{6,7},{7,6},{8,9},{9,8},{10,11... | collective-permute-start | bytes 1769480 | tf_op jit(solution)/shard_map/ppermute | solution.py:223
  75.6 0.7 pad_add_fusion.where_ref
  76.3 0.8 copy-done.8
  77.3 0.8 copy-done.10
  78.2 11.5 %all-to-all-done.r_ref = bf16[16,96,384]{2,1,0:T(8,128)(2,1)S(1)} async-done(((bf16[16,96,384]{2,1,0:T(8,128)(2,1)}), bf16[16,96,384]{2,1,0:T(8,128)(2,1)S(1)}, u32[]{:S(2)}, u32[]{:S(2)}) %all-to-all-start) | async-done | bytes 1179680 | tf_op jit(solution)/shard_map/all_to_all | solution.py:222
  89.6 1.0 copy-done
  90.7 6.6 %shard_map.49 = bf16[16,96,384]{2,1,0:T(8,128)(2,1)} custom-call(s32[2]{0:T(128)} %pad_add_fusion.where_ref, s32[32]{0:T(128)} %owner_ref.1, bf16[16,96,384]{2,1,0:T(8,128)(2,1)} %copy-done, bf16[192,1536]{1,0:T(8,128)(2,1)} %get-tuple-element.7.v0_ref.refs_0_, bf16[192,1536]{1,0:T(8,128)(2,1)} %get-tuple-element.8.v1_ref.refs_1_, ...), custom_call_target="tpu_custom_call" | custom-call | flops 2000000000 | bytes 7000000 | tf_op jit(solution)/shard_map/pallas_call | solution.py:224
  97.3 43.1 %all_to_all.10.x_ref = bf16[16,96,384]{2,1,0:T(8,128)(2,1)} all-to-all(bf16[16,96,384]{2,1,0:T(8,128)(2,1)} %shard_map.49), channel_id=1, replica_groups=mesh['grp'=16,'blk'=32] {'grp'}, dimensions={0} | all-to-all | bytes 2359296 | tf_op jit(solution)/shard_map/all_to_all | solution.py:229
  140.4 4.9 %shard_map.50 = bf16[42,84,128]{2,1,0:T(8,128)(2,1)} custom-call(s32[16]{0:T(128)} %start_ref.1, bf16[16,96,384]{2,1,0:T(8,128)(2,1)} %all_to_all.10.x_ref), custom_call_target="tpu_custom_call" | custom-call | flops 1000000000 | bytes 2000000 | tf_op jit(solution)/shard_map/pallas_call | solution.py:230
  (23 shorter events, 0.4 us)
Async XLA Ops:
  0.0 43.3 %collective-permute-start = (bf16[376,1504]{1,0:T(8,128)(2,1)}, bf16[376,1504]{1,0:T(8,128)(2,1)S(1)}, u32[]{:S(2)}, u32[]{:S(2)}) collective-permute-start(bf16[376,1504]{1,0:T(8,128)(2,1)} %bitcast.10), channel_id=1, source_target_pairs={{0,1},{1,0},{2,3},{3,2},{4,5},{5,4},{6,7},{7,6},{8,9},{9,8},{10,11... | collective-permute-start | bytes 3393032 | tf_op jit(solution)/shard_map/ppermute | solution.py:203
  36.2 14.4 %collective-permute-start.1 = (bf16[192,1536]{1,0:T(8,128)(2,1)}, bf16[192,1536]{1,0:T(8,128)(2,1)S(1)}, u32[]{:S(2)}, u32[]{:S(2)}) collective-permute-start(bf16[192,1536]{1,0:T(8,128)(2,1)} %get-tuple-element.7.v0_ref.refs_0_), channel_id=1, source_target_pairs={{0,16},{1,17},{2,18},{3,19},{4,20},{5,21},{6,22},{7,23},{8,24},{9,... | collective-permute-start | bytes 1769480 | tf_op jit(solution)/shard_map/ppermute | solution.py:210
  39.4 12.5 %collective-permute-start.2 = (bf16[192,1536]{1,0:T(8,128)(2,1)}, bf16[192,1536]{1,0:T(8,128)(2,1)S(1)}, u32[]{:S(2)}, u32[]{:S(2)}) collective-permute-start(bf16[192,1536]{1,0:T(8,128)(2,1)} %get-tuple-element.8.v1_ref.refs_1_), channel_id=1, source_target_pairs={{0,48},{1,49},{2,50},{3,51},{4,52},{5,53},{6,54},{7,55},{8,56},{9,... | collective-permute-start | bytes 1769480 | tf_op jit(solution)/shard_map/ppermute | solution.py:211
  43.3 1.1 copy-start.1
  50.6 1.3 copy-start.4
  51.9 0.8 copy-start.6
  59.1 7.8 %copy-start.2 = (bf16[192,1536]{1,0:T(8,128)(2,1)S(1)}, bf16[192,1536]{1,0:T(8,128)(2,1)}, u32[]{:S(2)}) copy-start(bf16[192,1536]{1,0:T(8,128)(2,1)} %get-tuple-element.7.v0_ref.refs_0_) | copy-start | bytes 1769476
  59.1 9.7 %copy-start.3 = (bf16[192,1536]{1,0:T(8,128)(2,1)S(1)}, bf16[192,1536]{1,0:T(8,128)(2,1)}, u32[]{:S(2)}) copy-start(bf16[192,1536]{1,0:T(8,128)(2,1)} %get-tuple-element.8.v1_ref.refs_1_) | copy-start | bytes 1769476
  59.1 12.2 %copy-start.5 = (bf16[192,1536]{1,0:T(8,128)(2,1)S(1)}, bf16[192,1536]{1,0:T(8,128)(2,1)}, u32[]{:S(2)}) copy-start(bf16[192,1536]{1,0:T(8,128)(2,1)} %copy-done.4) | copy-start | bytes 1769476
  59.1 14.1 %copy-start.7 = (bf16[192,1536]{1,0:T(8,128)(2,1)S(1)}, bf16[192,1536]{1,0:T(8,128)(2,1)}, u32[]{:S(2)}) copy-start(bf16[192,1536]{1,0:T(8,128)(2,1)} %copy-done.6) | copy-start | bytes 1769476
  59.1 30.5 %all-to-all-start = ((bf16[16,96,384]{2,1,0:T(8,128)(2,1)}), bf16[16,96,384]{2,1,0:T(8,128)(2,1)S(1)}, u32[]{:S(2)}, u32[]{:S(2)}) async-start(bf16[16,96,384]{2,1,0:T(8,128)(2,1)} %shard_map.48), calls=%async_computation | async-start | bytes 2359296 | tf_op jit(solution)/shard_map/all_to_all | solution.py:222
  66.9 9.4 %collective-permute-start.3 = (bf16[192,1536]{1,0:T(8,128)(2,1)S(1)}, bf16[192,1536]{1,0:T(8,128)(2,1)S(1)}, u32[]{:S(2)}, u32[]{:S(2)}) collective-permute-start(bf16[192,1536]{1,0:T(8,128)(2,1)S(1)} %copy-done.2), channel_id=1, source_target_pairs={{0,1},{1,0},{2,3},{3,2},{4,5},{5,4},{6,7},{7,6},{8,9},{9,8},{10,11... | collective-permute-start | bytes 1769480 | tf_op jit(solution)/shard_map/ppermute | solution.py:223
  68.8 7.5 %collective-permute-start.4 = (bf16[192,1536]{1,0:T(8,128)(2,1)S(1)}, bf16[192,1536]{1,0:T(8,128)(2,1)S(1)}, u32[]{:S(2)}, u32[]{:S(2)}) collective-permute-start(bf16[192,1536]{1,0:T(8,128)(2,1)S(1)} %copy-done.3), channel_id=1, source_target_pairs={{0,1},{1,0},{2,3},{3,2},{4,5},{5,4},{6,7},{7,6},{8,9},{9,8},{10,11... | collective-permute-start | bytes 1769480 | tf_op jit(solution)/shard_map/ppermute | solution.py:223
  71.3 5.0 %collective-permute-start.5 = (bf16[192,1536]{1,0:T(8,128)(2,1)S(1)}, bf16[192,1536]{1,0:T(8,128)(2,1)S(1)}, u32[]{:S(2)}, u32[]{:S(2)}) collective-permute-start(bf16[192,1536]{1,0:T(8,128)(2,1)S(1)} %copy-done.5), channel_id=1, source_target_pairs={{0,1},{1,0},{2,3},{3,2},{4,5},{5,4},{6,7},{7,6},{8,9},{9,8},{10,11... | collective-permute-start | bytes 1769480 | tf_op jit(solution)/shard_map/ppermute | solution.py:223
  73.2 5.0 %collective-permute-start.6 = (bf16[192,1536]{1,0:T(8,128)(2,1)S(1)}, bf16[192,1536]{1,0:T(8,128)(2,1)}, u32[]{:S(2)}, u32[]{:S(2)}) collective-permute-start(bf16[192,1536]{1,0:T(8,128)(2,1)S(1)} %copy-done.7), channel_id=1, source_target_pairs={{0,1},{1,0},{2,3},{3,2},{4,5},{5,4},{6,7},{7,6},{8,9},{9,8},{10,11... | collective-permute-start | bytes 1769480 | tf_op jit(solution)/shard_map/ppermute | solution.py:223
  76.3 0.8 copy-start.8
  76.3 1.0 copy-start.9
  77.3 0.8 copy-start.10
  89.6 1.1 copy-start
